TPU v7x, 512 devices: a whole 4x8x8 slice. The times are simulated.
512 devices in a mesh: frames: 64 (over y, x, core), coils: 8 (over z).
Axes of the slice: x: 4, y: 8, z: 8, core: 2. Of those that a mesh axis runs over, the one named last changes fastest.
Arguments:
- kspace: bfloat16 [64, 32, 2, 32, 256], P('frames', 'coils'), may hold values from -6 to 6
- sensitivity: bfloat16 [32, 2, 256, 256], P('coils'), may hold values from -3 to 3
- spoke_count: int32 [64], P('frames'), may hold values from 1 to 32, 1536 in all
- spoke_index: int32 [64, 32], P('frames'), may hold values from 0 to 32767
- band_offset: int32 [64, 32], P('frames'), may hold values from 0 to 252
- owner_map: int32 [8, 8192], replicated, may hold values from 0 to 8191, each once within a row
- aif: float32 [64], replicated, may hold values from 0.2 to 5
- ktrans: float32 [8, 8192], P('coils', 'frames'), may hold values from 0.02 to 0.4
- kep: float32 [8, 8192], P('coils', 'frames'), may hold values from 0.1 to 2
- baseline: float32 [2, 8, 8192], P(None, 'coils', 'frames'), may hold values from 0.5 to 2
Outputs:
- ktrans_new: float32 [8, 8192], P('coils', 'frames')
- kep_new: float32 [8, 8192], P('coils', 'frames')
- residual_images: bfloat16 [64, 2, 256, 256], P('frames', None, 'coils')
Inputs may be any that keep to these rules, and one draw needn't show every extreme that they name: `spoke_count`: spoke counts of all frames sum to 1536; some frame uses all 32 slots. `owner_map`: each row is a permutation of 0 to 8191.
All inputs are finite; a program needn't handle non-finite values. No bound on the sum of `spoke_count` on one device may be relied on, other than what follows from the above.
Results may differ from a plain program's by a relative error of at most 0.0074.
Values may be sent and summed in bfloat16 or wider, within the bound.
No kernel may reach another device: no remote copies, remote signals or barrier semaphores. Data moves between devices by JAX's collectives and lax.ppermute only.
A program may use at most 64 MiB of HBM per device.

v0:
```python
import math

import jax
import jax.numpy as jnp
from jax import lax
from jax.sharding import Mesh
from jax.sharding import PartitionSpec as P

FRAMES = ("frames_0", "frames_1", "frames_2")


KERNEL = (0.25, 0.75, 0.75, 0.25)
STEP_MINUTES = 0.05
DAMPING = 0.1


def cut_along(x, dim, count):
    dims = x.shape
    tiles = x.reshape(*dims[:dim], count, dims[dim] // count, *dims[dim + 1 :])
    return jnp.moveaxis(tiles, dim, 0)


def sum_at_owner(x, axis, dim):
    count = lax.axis_size(axis)
    tiles = lax.all_to_all(cut_along(x, dim, count), axis, 0, 0, tiled=True)
    return jnp.sum(tiles, axis=0)


def in_order(tiles, dim):
    dims = list(tiles.shape[1:])
    dims[dim] *= tiles.shape[0]
    return jnp.moveaxis(tiles, 0, dim).reshape(dims)


def moved_by_axis(tiles, axes, turns):
    inside = tiles.shape[1:]
    result = tiles.reshape(*(lax.axis_size(a) for a in axes), *inside)
    for k in turns:
        result = lax.all_to_all(result, axes[k], k, k, tiled=True)
    return result.reshape(-1, *inside)


def exchange_by_chip(x, groups, turns, split_dim, concat_dim):
    count = lax.axis_size(groups[0]) * lax.axis_size(groups[1])
    tiles = cut_along(x, split_dim, count)
    return in_order(moved_by_axis(tiles, groups, turns), concat_dim)


def dft_tables(length):
    index = jnp.arange(length, dtype=jnp.int32)
    phase = (index[:, None] * index[None, :] % length).astype(jnp.float32) * (
        2.0 * math.pi / length
    )
    norm = 1.0 / math.sqrt(length)
    cosine = (jnp.cos(phase) * norm).astype(jnp.bfloat16)
    sine = (jnp.sin(phase) * norm).astype(jnp.bfloat16)
    column_table = jnp.stack([jnp.stack([cosine, sine], 1), jnp.stack([-sine, cosine], 1)], 0)
    row_table = jnp.stack([jnp.stack([cosine, -sine], 1), jnp.stack([sine, cosine], 1)], 0)
    return (column_table, row_table)


def spoke_weights(count, offset, spoke_number, rows):
    spokes = offset.shape[0]
    row_ids = jnp.arange(rows, dtype=jnp.int32)
    band = jnp.zeros((rows, spokes), jnp.float32)
    for shift_b in range(len(KERNEL)):
        band = band + KERNEL[shift_b] * (row_ids[:, None] == offset[None, :] + shift_b).astype(
            jnp.float32
        )
    live = (jnp.arange(spokes, dtype=jnp.int32) < count).astype(jnp.float32)
    turn = (spoke_number * 40503 % 65536).astype(jnp.float32) * (2.0 * math.pi / 65536.0)
    w_cos = band * (live * jnp.cos(turn))[None, :]
    w_sin = band * (live * jnp.sin(turn))[None, :]
    return jnp.stack([jnp.stack([w_cos, -w_sin], 1), jnp.stack([w_sin, w_cos], 1)], 0).astype(
        jnp.bfloat16
    )


def aif_matrix(aif):
    length = aif.shape[0]
    index = jnp.arange(length, dtype=jnp.int32)
    lag = index[:, None] - index[None, :]
    table = jnp.take(aif, jnp.clip(lag, 0, length - 1))
    return jnp.where(lag >= 0, table, jnp.zeros_like(table)) * STEP_MINUTES


def tofts_step(images, aif, ktrans, kep, baseline):
    frames = images.shape[0]
    times = jnp.arange(frames, dtype=jnp.int32).astype(jnp.float32) * STEP_MINUTES
    toeplitz = aif_matrix(aif)
    decay = jnp.exp(-times[:, None] * kep[None, :])
    conc = jnp.dot(toeplitz, decay, precision=lax.Precision.HIGHEST)
    slope = jnp.dot(toeplitz, -times[:, None] * decay, precision=lax.Precision.HIGHEST)
    real_part = images[:, 0]
    imag_part = images[:, 1]
    base_r = baseline[0][None, :]
    base_i = baseline[1][None, :]
    scale = 1.0 + ktrans[None, :] * conc
    miss_r = real_part - base_r * scale
    miss_i = imag_part - base_i * scale
    power = baseline[0] * baseline[0] + baseline[1] * baseline[1]
    project = base_r * miss_r + base_i * miss_i
    h_aa = power * jnp.sum(conc * conc, 0)
    h_ab = power * ktrans * jnp.sum(conc * slope, 0)
    h_bb = power * ktrans * ktrans * jnp.sum(slope * slope, 0)
    g_a = jnp.sum(conc * project, 0)
    g_b = ktrans * jnp.sum(slope * project, 0)
    d_aa = (1.0 + DAMPING) * h_aa + 1.0
    d_bb = (1.0 + DAMPING) * h_bb + 1.0
    determinant = d_aa * d_bb - h_ab * h_ab
    kt_next = ktrans + (d_bb * g_a - h_ab * g_b) / determinant
    kp_next = kep + (d_aa * g_b - h_ab * g_a) / determinant
    conc_next = jnp.dot(
        toeplitz, jnp.exp(-times[:, None] * kp_next[None, :]), precision=lax.Precision.HIGHEST
    )
    scale_next = 1.0 + kt_next[None, :] * conc_next
    residual = jnp.stack([real_part - base_r * scale_next, imag_part - base_i * scale_next], 1)
    return (kt_next, kp_next, residual)


def full_partial(row_table, half, sensitivity):
    coil_image = jnp.einsum(
        "qypr,fcprx->fcqyx", row_table, half, preferred_element_type=jnp.float32
    )
    sens = sensitivity.astype(jnp.float32)[None]
    partial_r = jnp.sum(
        sens[:, :, 0] * coil_image[:, :, 0] + sens[:, :, 1] * coil_image[:, :, 1], 1
    )
    partial_i = jnp.sum(
        sens[:, :, 0] * coil_image[:, :, 1] - sens[:, :, 1] * coil_image[:, :, 0], 1
    )
    return jnp.stack([partial_r, partial_i], 1)


def shards(
    kspace,
    sensitivity,
    spoke_count,
    spoke_index,
    band_offset,
    owner_map,
    aif,
    ktrans,
    kep,
    baseline,
):
    frame_dev, coil_dev, _, spokes, width = kspace.shape
    n_coils = lax.axis_size("coils")
    slab_vox = owner_map.shape[1]
    vox_dev = ktrans.shape[1]
    column_table, row_table = dft_tables(width)
    weights = jax.vmap(spoke_weights, in_axes=(0, 0, 0, None))(
        spoke_count, band_offset, spoke_index, width
    )
    grid = jnp.einsum("fqxps,fcpsy->fcqxy", weights, kspace, preferred_element_type=jnp.float32)
    grid = grid.astype(jnp.bfloat16)
    half = jnp.einsum(
        "fcprk,pkqx->fcqrx", grid, column_table, preferred_element_type=jnp.float32
    ).astype(jnp.bfloat16)
    coil_row = lax.dynamic_index_in_dim(owner_map, lax.axis_index("coils"), 0, keepdims=False)
    partial_value = full_partial(row_table, half, sensitivity)
    summed = sum_at_owner(partial_value, "coils", 2)
    slab = summed.astype(jnp.bfloat16).reshape(frame_dev, 2, slab_vox)
    picked = jnp.take(slab, coil_row, axis=2)
    owned = exchange_by_chip(picked, (("frames_0", "frames_1"), "frames_2"), (1, 0), 2, 0)
    kt_next, kp_next, residual = tofts_step(
        owned.astype(jnp.float32), aif, ktrans[0], kep[0], baseline[:, 0]
    )
    returned = lax.all_to_all(
        residual.astype(jnp.bfloat16), FRAMES, split_axis=0, concat_axis=2, tiled=True
    )
    placed = jnp.zeros_like(returned).at[:, :, coil_row].set(returned)
    return (
        kt_next.reshape(1, vox_dev),
        kp_next.reshape(1, vox_dev),
        placed.reshape(frame_dev, 2, width // n_coils, width),
    )


def solution(mesh):
    split = Mesh(
        mesh.devices.reshape(8, 4, 2, mesh.shape["coils"]),
        ("frames_0", "frames_1", "frames_2", "coils"),
    )
    placed = (
        P(FRAMES, "coils", None, None, None),
        P("coils", None, None, None),
        P(FRAMES),
        P(FRAMES, None),
        P(FRAMES, None),
        P(),
        P(),
        P("coils", FRAMES),
        P("coils", FRAMES),
        P(None, "coils", FRAMES),
    )
    return jax.shard_map(
        shards,
        mesh=split,
        in_specs=placed,
        out_specs=(P("coils", FRAMES), P("coils", FRAMES), P(FRAMES, None, "coils", None)),
        check_vma=False,
    )
```

profile of v0, /device:TPU:1, one launch (start us, length us, event | category | flops | bytes accessed | tf_op | source)
XLA Modules:
  0.0 143.4 jit_solution(12544550501066917245)
XLA Ops:
  0.6 1.1 multiply_convert_fusion
  1.8 1.0 fusion.29
  3.4 0.7 broadcast_add_fusion.2
  4.1 1.5 %copy.87 = bf16[4,2,256,256]{2,3,1,0:T(8,128)(2,1)S(1)} copy(bf16[4,2,256,256]{3,2,1,0:T(8,128)(2,1)} %param.11) | data formatting | bytes 2097152 | tf_op args[1]
  5.6 0.2 bitcast_convert_fusion.2
  5.8 0.4 copy-done.4
  6.3 0.1 fusion.15
  6.4 0.1 negate_convert_fusion
  6.5 0.5 fusion
  7.0 0.7 fusion.1
  7.7 0.7 convolution_bitcast_fusion
  8.4 0.4 add_reduce_fusion
  8.8 0.1 copy.92
  9.0 0.1 copy.93
  9.2 0.8 copy.94
  10.0 10.8 %all-to-all-start = ((f32[8,1,2,32,256]{4,3,2,1,0:T(8,128)}), f32[8,1,2,32,256]{4,3,2,1,0:T(8,128)S(1)}, u32[]{:S(2)}, u32[]{:S(2)}) async-start(f32[8,1,2,32,256]{4,3,2,1,0:T(8,128)} %copy.94), calls=%async_computation | async-start | bytes 1048576 | tf_op jit(solution)/shard_map/all_to_all | solution.py:25
  20.9 1.0 compare_select_fusion
  22.0 24.7 %gather_fusion = f32[4096]{0:T(1024)S(1)} fusion(f32[64]{0:T(128)S(1)} %copy-done.1, s32[4096]{0:T(1024)S(1)} %broadcast_clamp_fusion.1), kind=kCustom, calls=%fused_computation | custom fusion | bytes 49152 | tf_op jit(solution)/shard_map/jit(_take)/gather | solution.py:83
  46.8 0.2 fusion.34
  47.1 1.1 copy.95
  48.2 29.2 %gather_fusion.1 = bf16[8192,2]{1,0:T(8,128)(2,1)} fusion(bf16[2,8192]{0,1:T(8,128)(2,1)S(1)} %bitcast.205, s32[8192]{0:T(1024)S(1)} %broadcast_clamp_fusion), kind=kCustom, calls=%fused_computation.1 | custom fusion | bytes 98304 | tf_op jit(solution)/shard_map/jit(_take)/gather | solution.py:164
  77.4 2.0 %copy.96 = bf16[1,2,64,128]{3,2,1,0:T(8,128)(2,1)S(1)} copy(bf16[1,2,64,128]{1,3,2,0:T(8,128)(2,1)} %bitcast.206) | data formatting | bytes 65536 | tf_op jit(solution)/shard_map/jit(_take)/gather | solution.py:164
  79.4 4.4 %all_to_all.33 = bf16[32,2,1,2,128]{4,0,3,2,1:T(8,128)(2,1)S(1)} all-to-all(bf16[32,2,1,2,128]{4,0,3,2,1:T(8,128)(2,1)S(1)} %copy.97), channel_id=1, replica_groups=mesh['frames_0'=8,'frames_1'=4,'frames_2'=2,'coils'=8] {'frames_2'}, dimensions={1} | all-to-all | bytes 65536 | tf_op jit(solution)/shard_map/all_to_all | solution.py:39
  83.8 0.6 copy.98
  84.5 9.7 %all-to-all-start.2 = ((bf16[32,2,1,2,128]{4,1,3,2,0:T(2,128)(2,1)}), bf16[32,2,1,2,128]{4,1,3,2,0:T(2,128)(2,1)S(1)}, u32[]{:S(2)}, u32[]{:S(2)}) async-start(bf16[32,2,1,2,128]{4,1,3,2,0:T(2,128)(2,1)} %copy.98), calls=%async_computation.2 | async-start | bytes 65536 | tf_op jit(solution)/shard_map/all_to_all | solution.py:39
  94.2 8.7 %all-to-all-done.2 = bf16[32,2,1,2,128]{4,1,3,2,0:T(2,128)(2,1)S(1)} async-done(((bf16[32,2,1,2,128]{4,1,3,2,0:T(2,128)(2,1)}), bf16[32,2,1,2,128]{4,1,3,2,0:T(2,128)(2,1)S(1)}, u32[]{:S(2)}, u32[]{:S(2)}) %all-to-all-start.2) | async-done | bytes 32800 | tf_op jit(solution)/shard_map/all_to_all | solution.py:39
  102.9 0.3 multiply_reduce_fusion.1
  103.2 0.2 fusion.39
  103.5 14.5 %all_to_all.34 = bf16[64,2,128]{2,1,0:T(2,128)(2,1)S(1)} all-to-all(bf16[64,2,128]{2,1,0:T(2,128)(2,1)S(1)} %copy.101), channel_id=1, replica_groups=mesh['frames_0'=8,'frames_1'=4,'frames_2'=2,'coils'=8] {'frames_0','fram..., dimensions={0} | all-to-all | bytes 65536 | tf_op jit(solution)/shard_map/all_to_all | solution.py:169
  118.0 1.9 %copy.102 = bf16[8192,2]{1,0:T(8,128)(2,1)} copy(bf16[8192,2]{0,1:T(2,128)(2,1)S(1)} %bitcast.209) | data formatting | bytes 65536 | tf_op jit(solution)/shard_map/all_to_all | solution.py:169
  119.9 21.9 %scatter_custom_fusion = bf16[2,8192]{0,1:T(8,128)(2,1)S(1)} fusion(s32[8192]{0:T(1024)S(1)} %bitcast.212, bf16[8192,2]{1,0:T(8,128)(2,1)} %copy.102, bf16[]{:T(256)} %constant.109.clone.1), kind=kCustom, calls=%fused_computation.14 | custom fusion | bytes 33280 | tf_op jit(solution)/shard_map/scatter | solution.py:172
  141.8 1.5 %copy.103 = bf16[1,2,32,256]{3,2,1,0:T(8,128)(2,1)} copy(bf16[1,2,32,256]{1,3,2,0:T(8,128)(2,1)S(1)} %bitcast.204) | data formatting | bytes 65536
  (37 shorter events, 0.5 us)
Async XLA Ops:
  0.6 5.9 %copy-start = (bf16[1,4,2,32,256]{4,3,2,1,0:T(8,128)(2,1)S(1)}, bf16[1,4,2,32,256]{4,3,2,1,0:T(8,128)(2,1)}, u32[]{:S(2)}) copy-start(bf16[1,4,2,32,256]{4,3,2,1,0:T(8,128)(2,1)} %param.10) | copy-start | bytes 393220
  5.6 0.7 copy-start.4
  5.6 0.8 copy-start.3
  8.8 13.1 %copy-start.1 = (f32[64]{0:T(128)S(1)}, f32[64]{0:T(128)}, u32[]{:S(2)}) copy-start(f32[64]{0:T(128)} %param.16) | copy-start | bytes 772
  10.0 37.1 %all-to-all-start = ((f32[8,1,2,32,256]{4,3,2,1,0:T(8,128)}), f32[8,1,2,32,256]{4,3,2,1,0:T(8,128)S(1)}, u32[]{:S(2)}, u32[]{:S(2)}) async-start(f32[8,1,2,32,256]{4,3,2,1,0:T(8,128)} %copy.94), calls=%async_computation | async-start | bytes 1048576 | tf_op jit(solution)/shard_map/all_to_all | solution.py:25
  21.9 24.8 %copy-start.5 = (f32[1,128]{1,0:T(1,128)S(1)}, f32[1,128]{1,0:T(1,128)}, u32[]{:S(2)}) copy-start(f32[1,128]{1,0:T(1,128)} %param.18) | copy-start | bytes 1540
  47.1 47.1 %copy-start.2 = (f32[2,1,128]{2,1,0:T(1,128)S(1)}, f32[2,1,128]{2,1,0:T(1,128)}, u32[]{:S(2)}) copy-start(f32[2,1,128]{2,1,0:T(1,128)} %param.19) | copy-start | bytes 3076
  47.1 55.8 %copy-start.6 = (f32[1,128]{1,0:T(1,128)S(1)}, f32[1,128]{1,0:T(1,128)}, u32[]{:S(2)}) copy-start(f32[1,128]{1,0:T(1,128)} %param.17) | copy-start | bytes 1540
  84.5 18.4 %all-to-all-start.2 = ((bf16[32,2,1,2,128]{4,1,3,2,0:T(2,128)(2,1)}), bf16[32,2,1,2,128]{4,1,3,2,0:T(2,128)(2,1)S(1)}, u32[]{:S(2)}, u32[]{:S(2)}) async-start(bf16[32,2,1,2,128]{4,1,3,2,0:T(2,128)(2,1)} %copy.98), calls=%async_computation.2 | async-start | bytes 65536 | tf_op jit(solution)/shard_map/all_to_all | solution.py:39
  103.2 38.6 %copy-start.7 = (f32[1,128]{1,0:T(1,128)}, f32[1,128]{1,0:T(1,128)S(1)}, u32[]{:S(2)}) copy-start(f32[1,128]{1,0:T(1,128)S(1)} %get-tuple-element.43) | copy-start | bytes 1540
  103.2 38.6 %copy-start.8 = (f32[1,128]{1,0:T(1,128)}, f32[1,128]{1,0:T(1,128)S(1)}, u32[]{:S(2)}) copy-start(f32[1,128]{1,0:T(1,128)S(1)} %get-tuple-element.44) | copy-start | bytes 1540
where the time goes:
time: 144 us; the launch traced here: 143 us
  local copies, waits for them, and re-layouts  86.3 us (60%)
  starting transfers between devices  20.5 us (14%)
  blocking collectives  18.8 us (13%)
  waiting for transfers between devices  8.68 us (6%)
  other arithmetic  4.74 us (3%)
  matrix products  2.65 us (2%)
  between operations  1.67 us (1%)
    gather x2, local copies, waits for them, and re-layouts, shards(): picked = jnp.take(slab, coil_row, axis=2)  31.2 us
    gather x2, local copies, waits for them, and re-layouts, aif_matrix(): table = jnp.take(aif, jnp.clip(lag, 0, length - 1))  24.8 us
    scatter x1, local copies, waits for them, and re-layouts, shards(): placed = jnp.zeros_like(returned).at[:, :, coil_row].set(returned)  21.9 us
    all_to_all x1, blocking collectives, shards(): lax.all_to_all(residual.astype(jnp.bfloat16), FRAMES, split_axis=0, conca...  14.5 us
    all_to_all x1, starting transfers between devices, sum_at_owner(): tiles = lax.all_to_all(cut_along(x, dim, count), axis, 0, 0, tiled=True)  10.8 us
    all_to_all x1, starting transfers between devices, moved_by_axis(): result = lax.all_to_all(result, axes[k], k, k, tiled=True)  9.67 us
    all_to_all x1, waiting for transfers between devices, moved_by_axis(): result = lax.all_to_all(result, axes[k], k, k, tiled=True)  8.68 us
    all_to_all x1, blocking collectives, moved_by_axis(): result = lax.all_to_all(result, axes[k], k, k, tiled=True)  4.35 us
  transfers between devices with their start and end apart: 2, of which 1 were waited for; matrix products, arithmetic and copies ran while one was open for 18% of the time, Pallas kernels for 0%

commit v1 on v0

v1 whole, which is shorter than its diff:
```python
import functools
import math

import jax
import jax.numpy as jnp
import numpy as np
from jax import lax
from jax.experimental import pallas as pl
from jax.experimental.pallas import tpu as pltpu
from jax.sharding import Mesh
from jax.sharding import PartitionSpec as P

FRAMES = ("frames_0", "frames_1", "frames_2")
STEP_MINUTES = 0.05
DAMPING = 0.1
BF16 = jnp.bfloat16
F32 = jnp.float32
MIB = 1 << 20


def dft_tables(length):
    index = np.arange(length)
    phase = (index[:, None] * index[None, :] % length) * (2.0 * math.pi / length)
    norm = 1.0 / math.sqrt(length)
    return np.stack([np.cos(phase) * norm, np.sin(phase) * norm]).astype(np.float32)


def iota(shape, dim, dtype=jnp.int32):
    return lax.broadcasted_iota(dtype, shape, dim)


def dot(a, b, contract=(1, 0), precision=None):
    return lax.dot_general(
        a,
        b,
        (((contract[0],), (contract[1],)), ((), ())),
        preferred_element_type=F32,
        precision=precision,
    )


def recon_kernel(
    count_ref,
    index_ref,
    offset_ref,
    kspace_hbm,
    sens_hbm,
    table_hbm,
    out_ref,
    kspace,
    sens,
    table,
    columns,
    rows,
    total,
    sems,
):
    coils, _, width = kspace.shape
    spokes = index_ref.shape[1]
    copy_k = pltpu.make_async_copy(kspace_hbm, kspace, sems.at[0])
    copy_t = pltpu.make_async_copy(table_hbm, table, sems.at[1])
    copy_s = [
        pltpu.make_async_copy(sens_hbm.at[c], sens.at[c], sems.at[2 + c]) for c in range(coils)
    ]
    copy_k.start()
    copy_t.start()
    for c in range(coils):
        copy_s[c].start()

    turn = (index_ref[...] * 40503 & 65535).astype(F32) * (2.0 * math.pi / 65536.0)
    live = (iota((1, spokes), 1) < count_ref[0]).astype(F32)
    cosine = live * jnp.cos(turn)
    sine = live * jnp.sin(turn)
    offset = offset_ref[...]
    top = jnp.concatenate([cosine, -sine], 1)
    low = jnp.concatenate([sine, cosine], 1)
    away = iota((width, 2 * spokes), 0) - jnp.concatenate([offset, offset], 1)
    band = jnp.where(
        (away == 0) | (away == 3), 0.25, jnp.where((away == 1) | (away == 2), 0.75, 0.0)
    )
    weights = jnp.concatenate([(band * top).astype(BF16), (band * low).astype(BF16)], 0)

    copy_t.wait()
    tc = table[0]
    ts = table[1]
    columns[:width, :width] = tc
    columns[:width, width:] = ts
    columns[width:, :width] = -ts
    columns[width:, width:] = tc
    rows[:width, :width] = tc
    rows[:width, width:] = -ts
    rows[width:, :width] = ts
    rows[width:, width:] = tc
    copy_k.wait()
    for c in range(coils):
        grid = dot(weights, kspace[c]).astype(BF16)
        half = dot(jnp.concatenate([grid[:width], grid[width:]], 1), columns[...]).astype(BF16)
        image = dot(rows[...], jnp.concatenate([half[:, :width], half[:, width:]], 0))
        copy_s[c].wait()
        sr = sens[c, 0].astype(F32)
        si = sens[c, 1].astype(F32)
        real = sr * image[:width] + si * image[width:]
        imag = sr * image[width:] - si * image[:width]
        if c > 0:
            real = real + total[0]
            imag = imag + total[1]
        if c < coils - 1:
            total[0] = real
            total[1] = imag
        else:
            slabs = out_ref.shape[0]
            deep = width // slabs
            for j in range(slabs):
                out_ref[j, :deep, :] = real[j * deep : (j + 1) * deep].astype(BF16)
                out_ref[j, deep:, :] = imag[j * deep : (j + 1) * deep].astype(BF16)


def recon(count, index, offset, kspace, sens, table, slabs):
    coils, pairs, width = kspace.shape
    vmem = pl.BlockSpec(memory_space=pltpu.VMEM)
    hbm = pl.BlockSpec(memory_space=pl.ANY)
    return pl.pallas_call(
        recon_kernel,
        out_shape=jax.ShapeDtypeStruct((slabs, 2 * width // slabs, width), BF16),
        in_specs=[pl.BlockSpec(memory_space=pltpu.SMEM), vmem, vmem, hbm, hbm, hbm],
        out_specs=vmem,
        scratch_shapes=[
            pltpu.VMEM((coils, pairs, width), BF16),
            pltpu.VMEM((coils, 2, width, width), BF16),
            pltpu.VMEM((2, width, width), BF16),
            pltpu.VMEM((2 * width, 2 * width), BF16),
            pltpu.VMEM((2 * width, 2 * width), BF16),
            pltpu.VMEM((2, width, width), F32),
            pltpu.SemaphoreType.DMA((2 + coils,)),
        ],
        compiler_params=pltpu.CompilerParams(vmem_limit_bytes=24 * MIB),
        name="recon",
    )(count, index, offset, kspace, sens, table)


def prepare_kernel(
    map_ref, aif_ref, ktrans_ref, kep_ref, base_ref, pick_ref, place_ref, slot_row_ref, lag_ref,
    conc_ref, slope_ref, solve_ref,
):
    width, slots = pick_ref.shape
    deep = slots // width
    frames = lag_ref.shape[0]
    row = map_ref[pl.ds(lax.axis_index("coils"), 1), :]
    block = 1024
    inverse = jnp.zeros((2 * deep, width), F32)
    for b in range(0, slots, block):
        part = row[:, b : b + block]
        pick = (iota((width, block), 0) == (part & (width - 1))).astype(F32).astype(BF16)
        pick_ref[:, b : b + block] = pick
        slot = iota((1, block), 1) + b
        here = iota((deep, block), 0) == (part // width)
        high = jnp.where(here, (slot // width).astype(F32), 0.0)
        low = jnp.where(here, (slot & (width - 1)).astype(F32), 0.0)
        digits = jnp.concatenate([high, low], 0).astype(BF16)
        inverse = inverse + dot(digits, pick, (1, 1))
    slot_row_ref[...] = inverse[:deep]
    low = inverse[deep:].astype(jnp.int32)
    for y in range(deep):
        place = (iota((width, width), 0) == low[y : y + 1]).astype(F32).astype(BF16)
        place_ref[:, y * width : (y + 1) * width] = place

    spread = jnp.broadcast_to(aif_ref[...], (frames, aif_ref.shape[1]))
    shifted = pltpu.roll(spread, 0, 1, stride=1, stride_axis=0)[:, :frames]
    early = iota((frames, frames), 1) >= iota((frames, frames), 0)
    lag = jnp.where(early, shifted, 0.0).T * STEP_MINUTES
    lag_ref[...] = lag
    times = iota((frames, 1), 0).astype(F32) * STEP_MINUTES
    ktrans = ktrans_ref[...]
    kep = kep_ref[...]
    decay = jnp.exp(-times * kep)
    conc = dot(lag, decay, precision=lax.Precision.HIGHEST)
    slope = dot(lag, -times * decay, precision=lax.Precision.HIGHEST)
    conc_ref[...] = conc
    slope_ref[...] = slope
    base_r = base_ref[0]
    base_i = base_ref[1]
    power = base_r * base_r + base_i * base_i
    h_aa = power * jnp.sum(conc * conc, 0, keepdims=True)
    h_ab = power * ktrans * jnp.sum(conc * slope, 0, keepdims=True)
    h_bb = power * ktrans * ktrans * jnp.sum(slope * slope, 0, keepdims=True)
    d_aa = (1.0 + DAMPING) * h_aa + 1.0
    d_bb = (1.0 + DAMPING) * h_bb + 1.0
    solve_ref[0:1, :] = d_aa
    solve_ref[1:2, :] = d_bb
    solve_ref[2:3, :] = h_ab
    solve_ref[3:4, :] = d_aa * d_bb - h_ab * h_ab


def prepare(owner_map, aif, ktrans, kep, baseline, width):
    slots = owner_map.shape[1]
    frames = aif.shape[0]
    own = ktrans.shape[1]
    lanes = -(-frames // 128) * 128
    aif_row = jnp.pad(aif, (0, lanes - frames)).reshape(1, lanes)
    vmem = pl.BlockSpec(memory_space=pltpu.VMEM)
    return pl.pallas_call(
        prepare_kernel,
        out_shape=(
            jax.ShapeDtypeStruct((width, slots), BF16),
            jax.ShapeDtypeStruct((width, slots), BF16),
            jax.ShapeDtypeStruct((slots // width, width), F32),
            jax.ShapeDtypeStruct((frames, frames), F32),
            jax.ShapeDtypeStruct((frames, own), F32),
            jax.ShapeDtypeStruct((frames, own), F32),
            jax.ShapeDtypeStruct((8, own), F32),
        ),
        in_specs=[vmem] * 5,
        out_specs=(vmem,) * 7,
        compiler_params=pltpu.CompilerParams(vmem_limit_bytes=24 * MIB),
        cost_estimate=pl.CostEstimate(flops=10**9, bytes_accessed=9 * MIB, transcendentals=10**4),
        name="prepare",
    )(owner_map, aif_row, ktrans, kep, baseline)


def pick_kernel(parts_ref, map_ref, pick_ref, out_ref, lines):
    width, slots = pick_ref.shape
    deep = slots // width
    lanes = out_ref.shape[1]
    total = parts_ref[0].astype(F32)
    for c in range(1, parts_ref.shape[0]):
        total = total + parts_ref[c].astype(F32)
    image = total.astype(BF16)
    row = map_ref[pl.ds(lax.axis_index("coils"), 1), :] // width
    block = 1024
    for b in range(0, slots, block):
        table = dot(image, pick_ref[:, b : b + block])
        here = iota((deep, block), 0) == row[:, b : b + block]
        for part in range(2):
            value = jnp.where(here, table[part * deep : (part + 1) * deep], 0.0)
            line = jnp.sum(value, 0, keepdims=True)
            for n in range(block // lanes):
                at = 2 * (b // lanes + n) + part
                lines[at : at + 1, :] = line[:, n * lanes : (n + 1) * lanes]
    out_ref[...] = lines[...].astype(BF16)


def pick_slots(parts, owner_map, pick, lanes):
    slots = owner_map.shape[1]
    vmem = pl.BlockSpec(memory_space=pltpu.VMEM)
    return pl.pallas_call(
        pick_kernel,
        out_shape=jax.ShapeDtypeStruct((2 * slots // lanes, lanes), BF16),
        in_specs=[vmem] * 3,
        out_specs=vmem,
        scratch_shapes=[pltpu.VMEM((2 * slots // lanes, lanes), F32)],
        compiler_params=pltpu.CompilerParams(vmem_limit_bytes=24 * MIB),
        name="pick",
    )(parts, owner_map, pick)


def step_kernel(
    owned_ref, lag_ref, conc_ref, slope_ref, solve_ref, ktrans_ref, kep_ref, base_ref,
    ktrans_out, kep_out, out_ref, lines,
):
    frames = lag_ref.shape[0]
    lines[...] = owned_ref[...].astype(F32)
    real = lines[pl.ds(0, frames, stride=2), :]
    imag = lines[pl.ds(1, frames, stride=2), :]
    ktrans = ktrans_ref[...]
    kep = kep_ref[...]
    base_r = base_ref[0]
    base_i = base_ref[1]
    conc = conc_ref[...]
    slope = slope_ref[...]
    scale = 1.0 + ktrans * conc
    project = base_r * (real - base_r * scale) + base_i * (imag - base_i * scale)
    g_a = jnp.sum(conc * project, 0, keepdims=True)
    g_b = ktrans * jnp.sum(slope * project, 0, keepdims=True)
    d_aa = solve_ref[0:1, :]
    d_bb = solve_ref[1:2, :]
    h_ab = solve_ref[2:3, :]
    determinant = solve_ref[3:4, :]
    kt_next = ktrans + (d_bb * g_a - h_ab * g_b) / determinant
    kp_next = kep + (d_aa * g_b - h_ab * g_a) / determinant
    ktrans_out[...] = kt_next
    kep_out[...] = kp_next
    times = iota((frames, 1), 0).astype(F32) * STEP_MINUTES
    decay = jnp.exp(-times * kp_next)
    scale = 1.0 + kt_next * dot(lag_ref[...], decay, precision=lax.Precision.HIGHEST)
    lines[pl.ds(0, frames, stride=2), :] = real - base_r * scale
    lines[pl.ds(1, frames, stride=2), :] = imag - base_i * scale
    out_ref[...] = lines[...].astype(BF16)


def tofts_step(owned, model, ktrans, kep, baseline):
    own = ktrans.shape[1]
    vmem = pl.BlockSpec(memory_space=pltpu.VMEM)
    return pl.pallas_call(
        step_kernel,
        out_shape=(
            jax.ShapeDtypeStruct((1, own), F32),
            jax.ShapeDtypeStruct((1, own), F32),
            jax.ShapeDtypeStruct(owned.shape, BF16),
        ),
        in_specs=[vmem] * 8,
        out_specs=(vmem,) * 3,
        scratch_shapes=[pltpu.VMEM(owned.shape, F32)],
        compiler_params=pltpu.CompilerParams(vmem_limit_bytes=8 * MIB),
        name="step",
    )(owned, *model, ktrans, kep, baseline)


def place_kernel(returned_ref, place_ref, slot_row_ref, out_ref, lines, image):
    width, slots = place_ref.shape
    deep = slots // width
    lines[...] = returned_ref[...].astype(F32)
    halves = [
        [lines[pl.ds(part + 2 * side, deep, stride=4), :] for side in range(2)] for part in range(2)
    ]
    source = jnp.concatenate([jnp.concatenate(h, 1) for h in halves], 0).astype(BF16)
    across = 4
    for y in range(0, deep, across):
        table = dot(source, place_ref[:, y * width : (y + across) * width])
        for n in range(across):
            which = slot_row_ref[y + n : y + n + 1, :]
            here = iota((deep, width), 0).astype(F32) == which
            for part in range(2):
                values = table[part * deep : (part + 1) * deep, n * width : (n + 1) * width]
                line = jnp.sum(jnp.where(here, values, 0.0), 0, keepdims=True)
                image[part * deep + y + n : part * deep + y + n + 1, :] = line
    out_ref[...] = image[...].astype(BF16)


def place_voxels(returned, place, slot_row):
    width, slots = place.shape
    deep = slots // width
    vmem = pl.BlockSpec(memory_space=pltpu.VMEM)
    return pl.pallas_call(
        place_kernel,
        out_shape=jax.ShapeDtypeStruct((2 * deep, width), BF16),
        in_specs=[vmem] * 3,
        out_specs=vmem,
        scratch_shapes=[pltpu.VMEM(returned.shape, F32), pltpu.VMEM((2 * deep, width), F32)],
        compiler_params=pltpu.CompilerParams(vmem_limit_bytes=24 * MIB),
        name="place",
    )(returned, place, slot_row)


def shards(
    kspace,
    sensitivity,
    spoke_count,
    spoke_index,
    band_offset,
    owner_map,
    aif,
    ktrans,
    kep,
    baseline,
    table,
):
    _, coils, _, spokes, width = kspace.shape
    slabs = lax.axis_size("coils")
    own = ktrans.shape[1]
    parts = recon(
        spoke_count,
        spoke_index,
        band_offset,
        kspace.reshape(coils, 2 * spokes, width),
        sensitivity,
        table,
        slabs,
    )
    parts = lax.all_to_all(parts, "coils", 0, 0, tiled=True)
    pick, place, slot_row, *model = prepare(owner_map, aif, ktrans, kep, baseline, width)
    picked = pick_slots(parts, owner_map, pick, own)
    owned = lax.all_to_all(picked.reshape(-1, 2, own), FRAMES, 0, 0, tiled=True)
    kt_next, kp_next, residual = tofts_step(owned.reshape(-1, own), model, ktrans, kep, baseline)
    returned = lax.all_to_all(residual.reshape(-1, 2, own), FRAMES, 0, 0, tiled=True)
    placed = place_voxels(returned.reshape(-1, own), place, slot_row)
    return kt_next, kp_next, placed.reshape(1, 2, width // slabs, width)


def solution(mesh):
    split = Mesh(
        mesh.devices.reshape(8, 4, 2, mesh.shape["coils"]),
        ("frames_0", "frames_1", "frames_2", "coils"),
    )
    placed = (
        P(FRAMES, "coils", None, None, None),
        P("coils", None, None, None),
        P(FRAMES),
        P(FRAMES, None),
        P(FRAMES, None),
        P(),
        P(),
        P("coils", FRAMES),
        P("coils", FRAMES),
        P(None, "coils", FRAMES),
    )
    mapped = jax.shard_map(
        shards,
        mesh=split,
        in_specs=(*placed, P()),
        out_specs=(P("coils", FRAMES), P("coils", FRAMES), P(FRAMES, None, "coils", None)),
        check_vma=False,
    )

    def step(kspace, *rest):
        table = jnp.asarray(dft_tables(kspace.shape[-1])).astype(BF16)
        return mapped(kspace, *rest, table)

    return step
```

time: 144 us -> 72.5 us (0.50)
  local copies, waits for them, and re-layouts: 86.3 us -> 14.1 us
  blocking collectives: 18.8 us -> 34.3 us
  Pallas kernels: 0 us -> 11.4 us
  starting transfers between devices: 20.5 us -> 10.9 us
  waiting for transfers between devices: 8.68 us -> 0.01 us
  other arithmetic: 4.74 us -> 0 us
  matrix products: 2.65 us -> 0 us
    gather x4 -> x0, local copies, waits for them, and re-layouts: 56 us -> none  [the longest x2 31.2 us: shards(): picked = jnp.take(slab, coil_row, axis=2)]
    scatter x1 -> x0, local copies, waits for them, and re-layouts: 21.9 us -> none  [shards(): placed = jnp.zeros_like(returned).at[:, :, coil_row].set(returned)]
    all_to_all x2, blocking collectives: 18.8 us -> 34.3 us  [the longest x1 20.9 us: shards(): owned = lax.all_to_all(picked.reshape(-1, 2, own), FRAMES, 0, 0, tiled=True)]
    pallas_call x0 -> x5, Pallas kernels: none -> 11.4 us  [the longest x1 4.62 us: recon(): pl.pallas_call(recon_kernel, out_shape=jax.ShapeDtypeStruct((slabs, 2 * w...]
    unnamed x20 -> x34, local copies, waits for them, and re-layouts: 3.5 us -> 13.4 us
    all_to_all x2 -> x1, starting transfers between devices: 20.5 us -> 10.9 us  [shards(): parts = lax.all_to_all(parts, 'coils', 0, 0, tiled=True)]
    all_to_all x2 -> x1, waiting for transfers between devices: 8.68 us -> 0.01 us  [shards(): parts = lax.all_to_all(parts, 'coils', 0, 0, tiled=True)]
    dot_general x6 -> x0, matrix products: 2.65 us -> none  [the longest x1 0.74 us: shards(): jnp.einsum('fcprk,pkqx->fcqrx', grid, column_table, preferred_element_typ...]
  transfers between devices with their start and end apart: 2 -> 1, of which waited for: 1 -> 0; matrix products, arithmetic and copies ran while one was open for 18% -> 1% of each run, Pallas kernels for 0% -> 5%
where the time goes in v1:
time: 72.5 us; the launch traced here: 72.1 us
  blocking collectives  34.3 us (47%)
  local copies, waits for them, and re-layouts  14.1 us (19%)
  Pallas kernels  11.4 us (16%)
  starting transfers between devices  10.9 us (15%)
  between operations  1.33 us (2%)
    all_to_all x1, blocking collectives, shards(): owned = lax.all_to_all(picked.reshape(-1, 2, own), FRAMES, 0, 0, tiled=True)  20.9 us
    unnamed x34, local copies, waits for them, and re-layouts  13.4 us
    all_to_all x1, blocking collectives, shards(): lax.all_to_all(residual.reshape(-1, 2, own), FRAMES, 0, 0, tiled=True)  13.4 us
    all_to_all x1, starting transfers between devices, shards(): parts = lax.all_to_all(parts, 'coils', 0, 0, tiled=True)  10.9 us
    pallas_call x1, Pallas kernels, recon(): pl.pallas_call(recon_kernel, out_shape=jax.ShapeDtypeStruct((slabs, 2 * w...  4.62 us
    pallas_call x1, Pallas kernels, prepare(): pl.pallas_call(prepare_kernel, out_shape=(jax.ShapeDtypeStruct((width, sl...  3.8 us
    pallas_call x1, Pallas kernels, place_voxels(): pl.pallas_call(place_kernel, out_shape=jax.ShapeDtypeStruct((2 * deep, wi...  1.49 us
  transfers between devices with their start and end apart: 1, of which 0 were waited for; matrix products, arithmetic and copies ran while one was open for 1% of the time, Pallas kernels for 5%

profile of v1, /device:TPU:1, one launch (start us, length us, event | category | flops | bytes accessed | tf_op | source)
XLA Modules:
  0.0 72.1 jit_solution(17573393953957274084)
XLA Ops:
  1.3 0.0 copy-start.4
  1.3 1.2 %copy-done.4 = bf16[4,2,256,256]{3,2,1,0:T(8,128)(2,1)S(1)} copy-done((bf16[4,2,256,256]{3,2,1,0:T(8,128)(2,1)S(1)}, bf16[4,2,256,256]{3,2,1,0:T(8,128)(2,1)}, u32[]{:S(2)}) %copy-start.4) | copy-done | bytes 1048600
  2.5 0.0 copy-start.7
  2.5 0.9 %copy-done.7 = bf16[2,256,256]{2,1,0:T(8,128)(2,1)S(1)} copy-done((bf16[2,256,256]{2,1,0:T(8,128)(2,1)S(1)}, bf16[2,256,256]{2,1,0:T(8,128)(2,1)}, u32[]{:S(2)}) %copy-start.7) | copy-done | bytes 262168
  3.5 0.9 %copy-done.8 = bf16[1,4,2,32,256]{4,3,2,1,0:T(8,128)(2,1)S(1)} copy-done((bf16[1,4,2,32,256]{4,3,2,1,0:T(8,128)(2,1)S(1)}, bf16[1,4,2,32,256]{4,3,2,1,0:T(8,128)(2,1)}, u32[]{:S(2)}) %copy-start.8) | copy-done | bytes 131096
  4.4 0.0 copy-start.11
  4.4 0.7 copy-done.11
  5.0 0.0 copy-start.12
  5.0 0.7 copy-done.12
  5.7 4.6 %recon.1 = bf16[8,64,256]{2,1,0:T(8,128)(2,1)} custom-call(s32[1]{0:T(128)S(6)} %copy.14.count_ref, s32[1,32]{1,0:T(1,128)S(1)} %copy-done.11, s32[1,32]{1,0:T(1,128)S(1)} %copy-done.12, bf16[4,64,256]{2,1,0:T(8,128)(2,1)S(1)} %bitcast.11, bf16[4,2,256,256]{3,2,1,0:T(8,128)(2,1)S(1)} %copy-done.4, bf16[2,256,256]{2,1,0:T(8,128)(2,1)S(1)} %copy-done.7), custom_call_target="tpu_custom_call" | custom-call | tf_op jit(solution)/shard_map/recon/pallas_call | solution.py:122
  10.3 10.9 %all-to-all-start = ((bf16[8,64,256]{2,1,0:T(8,128)(2,1)}), bf16[8,64,256]{2,1,0:T(8,128)(2,1)S(1)}, u32[]{:S(2)}, u32[]{:S(2)}) async-start(bf16[8,64,256]{2,1,0:T(8,128)(2,1)} %recon.1), calls=%async_computation | async-start | bytes 524288 | tf_op jit(solution)/shard_map/all_to_all | solution.py:369
  21.2 0.7 pad_bitcast_fusion.aif_ref
  21.8 0.9 %copy-done.5 = s32[8,8192]{1,0:T(8,128)S(1)} copy-done((s32[8,8192]{1,0:T(8,128)S(1)}, s32[8,8192]{1,0:T(8,128)}, u32[]{:S(2)}) %copy-start.5) | copy-done | bytes 262168
  22.8 0.7 copy-done.9
  23.5 0.7 copy-done.13
  24.1 0.7 copy-done.15
  24.8 3.8 %prepare.1 = (bf16[256,8192]{1,0:T(8,128)(2,1)S(1)}, bf16[256,8192]{1,0:T(8,128)(2,1)S(1)}, f32[32,256]{1,0:T(8,128)S(1)}, f32[64,64]{1,0:T(8,128)S(1)}, f32[64,...) custom-call(s32[8,8192]{1,0:T(8,128)S(1)} %copy-done.5, f32[1,128]{1,0:T(1,128)S(1)} %pad_bitcast_fusion.aif_ref, ...), custom_call_target="tpu_custom_call" | custom-call | flops 1000000000 | bytes 9437184 | tf_op jit(solution)/shard_map/prepare/pallas_call | solution.py:201
  28.6 0.0 copy-start
  28.6 1.9 %copy-done = bf16[256,8192]{1,0:T(8,128)(2,1)} copy-done((bf16[256,8192]{1,0:T(8,128)(2,1)}, bf16[256,8192]{1,0:T(8,128)(2,1)S(1)}, u32[]{:S(2)}) %copy-start) | copy-done | bytes 4194328
  30.5 2.0 %copy-done.2 = bf16[256,8192]{1,0:T(8,128)(2,1)} copy-done((bf16[256,8192]{1,0:T(8,128)(2,1)}, bf16[256,8192]{1,0:T(8,128)(2,1)S(1)}, u32[]{:S(2)}) %copy-start.2) | copy-done | bytes 4194328
  32.5 0.0 all-to-all-done.parts_ref
  32.5 0.0 copy-done.6
  32.5 2.2 %copy-done.1 = bf16[256,8192]{1,0:T(8,128)(2,1)S(1)} copy-done((bf16[256,8192]{1,0:T(8,128)(2,1)S(1)}, bf16[256,8192]{1,0:T(8,128)(2,1)}, u32[]{:S(2)}) %copy-start.1) | copy-done | bytes 4194328
  34.7 0.9 %pick.1 = bf16[128,128]{1,0:T(8,128)(2,1)S(1)} custom-call(bf16[8,64,256]{2,1,0:T(8,128)(2,1)S(1)} %all-to-all-done.parts_ref, s32[8,8192]{1,0:T(8,128)S(1)} %copy-done.6, bf16[256,8192]{1,0:T(8,128)(2,1)S(1)} %copy-done.1), custom_call_target="tpu_custom_call" | custom-call | tf_op jit(solution)/shard_map/pick/pallas_call | solution.py:245
  35.6 20.9 %all_to_all.15 = bf16[64,2,128]{2,1,0:T(2,128)(2,1)S(1)} all-to-all(bf16[64,2,128]{2,1,0:T(2,128)(2,1)S(1)} %bitcast.9), channel_id=1, replica_groups=mesh['frames_0'=8,'frames_1'=4,'frames_2'=2,'coils'=8] {'frames_0','fram..., dimensions={0} | all-to-all | bytes 65536 | tf_op jit(solution)/shard_map/all_to_all | solution.py:372
  56.5 0.0 copy-done.10
  56.5 0.0 copy-done.14
  56.5 0.0 copy-done.16
  56.5 0.6 step.1
  57.1 13.4 %all_to_all.16 = bf16[64,2,128]{2,1,0:T(2,128)(2,1)S(1)} all-to-all(bf16[64,2,128]{2,1,0:T(2,128)(2,1)S(1)} %bitcast.12), channel_id=1, replica_groups=mesh['frames_0'=8,'frames_1'=4,'frames_2'=2,'coils'=8] {'frames_0','fram..., dimensions={0} | all-to-all | bytes 65536 | tf_op jit(solution)/shard_map/all_to_all | solution.py:374
  70.6 0.0 copy-done.3
  70.6 1.5 %place.1 = bf16[64,256]{1,0:T(8,128)(2,1)} custom-call(bf16[128,128]{1,0:T(8,128)(2,1)S(1)} %bitcast.8, bf16[256,8192]{1,0:T(8,128)(2,1)S(1)} %copy-done.3, f32[32,256]{1,0:T(8,128)S(1)} %get-tuple-element.22.slot_row_ref), custom_call_target="tpu_custom_call" | custom-call | tf_op jit(solution)/shard_map/place/pallas_call | solution.py:333
  (12 shorter events, 0.0 us)
Async XLA Ops:
  1.3 1.2 %copy-start.4 = (bf16[4,2,256,256]{3,2,1,0:T(8,128)(2,1)S(1)}, bf16[4,2,256,256]{3,2,1,0:T(8,128)(2,1)}, u32[]{:S(2)}) copy-start(bf16[4,2,256,256]{3,2,1,0:T(8,128)(2,1)} %sens_hbm.1) | copy-start | bytes 3145732
  2.5 0.9 %copy-start.7 = (bf16[2,256,256]{2,1,0:T(8,128)(2,1)S(1)}, bf16[2,256,256]{2,1,0:T(8,128)(2,1)}, u32[]{:S(2)}) copy-start(bf16[2,256,256]{2,1,0:T(8,128)(2,1)} %constant.6.clone.table_hbm) | copy-start | bytes 786436
  3.5 0.9 %copy-start.8 = (bf16[1,4,2,32,256]{4,3,2,1,0:T(8,128)(2,1)S(1)}, bf16[1,4,2,32,256]{4,3,2,1,0:T(8,128)(2,1)}, u32[]{:S(2)}) copy-start(bf16[1,4,2,32,256]{4,3,2,1,0:T(8,128)(2,1)} %param.11) | copy-start | bytes 393220
  4.4 0.7 copy-start.11
  5.0 0.7 copy-start.12
  5.7 26.8 %copy-start.6 = (s32[8,8192]{1,0:T(8,128)S(1)}, s32[8,8192]{1,0:T(8,128)}, u32[]{:S(2)}) copy-start(s32[8,8192]{1,0:T(8,128)} %map_ref.3) | copy-start | bytes 786436
  10.3 22.2 %all-to-all-start = ((bf16[8,64,256]{2,1,0:T(8,128)(2,1)}), bf16[8,64,256]{2,1,0:T(8,128)(2,1)S(1)}, u32[]{:S(2)}, u32[]{:S(2)}) async-start(bf16[8,64,256]{2,1,0:T(8,128)(2,1)} %recon.1), calls=%async_computation | async-start | bytes 524288 | tf_op jit(solution)/shard_map/all_to_all | solution.py:369
  21.8 0.9 %copy-start.5 = (s32[8,8192]{1,0:T(8,128)S(1)}, s32[8,8192]{1,0:T(8,128)}, u32[]{:S(2)}) copy-start(s32[8,8192]{1,0:T(8,128)} %map_ref.3) | copy-start | bytes 786436
  22.8 0.7 copy-start.9
  23.5 0.7 copy-start.13
  24.1 0.7 copy-start.15
  24.8 31.8 %copy-start.10 = (f32[2,1,128]{2,1,0:T(1,128)S(1)}, f32[2,1,128]{2,1,0:T(1,128)}, u32[]{:S(2)}) copy-start(f32[2,1,128]{2,1,0:T(1,128)} %base_ref.3) | copy-start | bytes 3076
  24.8 31.8 %copy-start.14 = (f32[1,128]{1,0:T(1,128)S(1)}, f32[1,128]{1,0:T(1,128)}, u32[]{:S(2)}) copy-start(f32[1,128]{1,0:T(1,128)} %ktrans_ref.3) | copy-start | bytes 1540
  24.8 31.8 %copy-start.16 = (f32[1,128]{1,0:T(1,128)S(1)}, f32[1,128]{1,0:T(1,128)}, u32[]{:S(2)}) copy-start(f32[1,128]{1,0:T(1,128)} %kep_ref.3) | copy-start | bytes 1540
  28.6 2.0 %copy-start = (bf16[256,8192]{1,0:T(8,128)(2,1)}, bf16[256,8192]{1,0:T(8,128)(2,1)S(1)}, u32[]{:S(2)}) copy-start(bf16[256,8192]{1,0:T(8,128)(2,1)S(1)} %get-tuple-element.13.pick_ref) | copy-start | bytes 12582916
  30.5 2.0 %copy-start.2 = (bf16[256,8192]{1,0:T(8,128)(2,1)}, bf16[256,8192]{1,0:T(8,128)(2,1)S(1)}, u32[]{:S(2)}) copy-start(bf16[256,8192]{1,0:T(8,128)(2,1)S(1)} %get-tuple-element.21.place_ref) | copy-start | bytes 12582916
  32.5 2.2 %copy-start.1 = (bf16[256,8192]{1,0:T(8,128)(2,1)S(1)}, bf16[256,8192]{1,0:T(8,128)(2,1)}, u32[]{:S(2)}) copy-start(bf16[256,8192]{1,0:T(8,128)(2,1)} %copy-done) | copy-start | bytes 12582916
  34.7 35.9 %copy-start.3 = (bf16[256,8192]{1,0:T(8,128)(2,1)S(1)}, bf16[256,8192]{1,0:T(8,128)(2,1)}, u32[]{:S(2)}) copy-start(bf16[256,8192]{1,0:T(8,128)(2,1)} %copy-done.2) | copy-start | bytes 12582916
